TPU v7x, 128 devices: a whole 4x4x4 slice. The times are simulated.
128 devices in a mesh: row: 8 (over y, x_lo), col: 16 (over x_hi, z, core).
Axes of the slice: x: 4 (x_hi: 2, x_lo: 2; x = x_hi * 2 + x_lo), y: 4, z: 4, core: 2. Of those that a mesh axis runs over, the one named last changes fastest.
Arguments:
- activations: bfloat16 [2048, 8192], P('col', 'row'), may hold values from -6 to 6
- output_grad: bfloat16 [2048, 8192], P('col', 'row'), may hold values from -1.5 to 1.5
- tile_counts: int32 [32], replicated, may hold values from 16 to 64, as said below
- w_gate: bfloat16 [8192, 15360], P('row', 'col'), may hold values from -0.0625 to 0.0625
- w_up: bfloat16 [8192, 15360], P('row', 'col'), may hold values from -0.0625 to 0.0625
- w_down: bfloat16 [15360, 8192], P('col', 'row'), may hold values from -0.046875 to 0.046875
Outputs:
- input_grad: bfloat16 [2048, 8192], P('col', 'row')
- grad_gate: bfloat16 [8192, 15360], P('row', 'col')
- grad_up: bfloat16 [8192, 15360], P('row', 'col')
- grad_down: bfloat16 [15360, 8192], P('col', 'row')
Inputs may be any that keep to these rules, and one draw needn't show every extreme that they name: `tile_counts`: number of live tokens at the start of each tile of 64 positions; some tile is full and some holds 16.
All inputs are finite; a program needn't handle non-finite values.
Results may differ from a plain program's by a relative error of at most 0.03.
Values may be sent and summed in bfloat16 or wider, within the bound.
No kernel may reach another device: no remote copies, remote signals or barrier semaphores. Data moves between devices by JAX's collectives and lax.ppermute only.
A program may use at most 128 MiB of HBM per device.

v0:
```python
import jax
import jax.numpy as jnp
from jax import lax
from jax.sharding import PartitionSpec as P

TILE = 64


def contract_rows(left, right):
    return lax.dot_general(
        left, right, (((0,), (0,)), ((), ())), preferred_element_type=jnp.float32
    )


def contract_cols(left, right):
    return lax.dot_general(
        left, right, (((1,), (1,)), ((), ())), preferred_element_type=jnp.float32
    )


def swiglu_back(totals, columns):
    gate_sum = totals[:, :columns]
    up_sum = totals[:, columns : 2 * columns]
    back_sum = totals[:, 2 * columns :]
    sigmoid_gate = jax.nn.sigmoid(gate_sum)
    hidden = (gate_sum * sigmoid_gate * up_sum).astype(jnp.bfloat16)
    d_gate = (back_sum * up_sum * sigmoid_gate * (1.0 + gate_sum * (1.0 - sigmoid_gate))).astype(
        jnp.bfloat16
    )
    d_up = (back_sum * gate_sum * sigmoid_gate).astype(jnp.bfloat16)
    return (hidden, d_gate, d_up)


def shards(activations, output_grad, tile_counts, w_gate, w_up, w_down):
    own_rows = activations.shape[0]
    columns = w_gate.shape[1]
    tile_total = tile_counts.shape[0]
    position = lax.axis_index("col") * own_rows + lax.iota(jnp.int32, own_rows)
    in_tile = (position // TILE)[:, None] == lax.iota(jnp.int32, tile_total)[None, :]
    row_limit = jnp.sum(jnp.where(in_tile, tile_counts[None, :], 0), axis=1)
    kept_rows = position % TILE < row_limit
    live_grad = jnp.where(kept_rows[:, None], output_grad, jnp.zeros_like(output_grad))
    inputs_all, grads_all = (
        lax.all_gather(activations, "col", axis=0, tiled=True),
        lax.all_gather(live_grad, "col", axis=0, tiled=True),
    )
    gate_part = jnp.dot(inputs_all, w_gate, preferred_element_type=jnp.float32)
    up_part = jnp.dot(inputs_all, w_up, preferred_element_type=jnp.float32)
    back_part = contract_cols(grads_all, w_down)
    totals = lax.psum_scatter(
        jnp.concatenate([gate_part, up_part, back_part], axis=1).astype(jnp.bfloat16),
        "row",
        scatter_dimension=0,
        tiled=True,
    ).astype(jnp.float32)
    hidden_share, gate_share, up_share = swiglu_back(totals, columns)
    hidden, d_gate, d_up = (
        lax.all_gather(hidden_share, "row", axis=0, tiled=True),
        lax.all_gather(gate_share, "row", axis=0, tiled=True),
        lax.all_gather(up_share, "row", axis=0, tiled=True),
    )
    grad_gate = contract_rows(inputs_all, d_gate).astype(jnp.bfloat16)
    grad_up = contract_rows(inputs_all, d_up).astype(jnp.bfloat16)
    grad_down = contract_rows(hidden, grads_all).astype(jnp.bfloat16)
    input_grad = lax.psum_scatter(
        (contract_cols(d_gate, w_gate) + contract_cols(d_up, w_up)).astype(jnp.bfloat16),
        "col",
        scatter_dimension=0,
        tiled=True,
    )
    return (input_grad, grad_gate, grad_up, grad_down)


def solution(mesh):
    in_specs = (
        P("col", "row"),
        P("col", "row"),
        P(),
        P("row", "col"),
        P("row", "col"),
        P("col", "row"),
    )
    out_specs = (P("col", "row"), P("row", "col"), P("row", "col"), P("col", "row"))
    return jax.shard_map(shards, mesh=mesh, in_specs=in_specs, out_specs=out_specs, check_vma=False)
```

profile of v0, /device:TPU:0, one launch (start us, length us, event | category | flops | bytes accessed | tf_op | source)
XLA Modules:
  0.0 740.1 jit_solution(12108002158446484)
XLA Ops:
  7.2 0.7 all-gather.6.cloned.1.call-update
  8.0 0.7 select_reduce_fusion
  8.7 1.7 broadcast_select_fusion
  10.6 57.9 %all-gather.6.cloned.1.call-done = bf16[2048,1024]{1,0:T(8,128)(2,1)} async-done(((bf16[128,1024]{1,0:T(8,128)(2,1)}), bf16[2048,1024]{1,0:T(8,128)(2,1)}) %all-gather.6.cloned.1.call-update) | async-done | bytes 4194320 | tf_op jit(solution)/shard_map/all_gather | solution.py:44
  68.4 9.1 %convolution_convert_fusion.1 = bf16[2048,960]{0,1:T(8,128)(2,1)} fusion(bf16[2048,1024]{1,0:T(8,128)(2,1)} %all-gather.6.cloned.1.call-done, bf16[1024,960]{0,1:T(8,128)(2,1)} %param.10), kind=kOutput, calls=%fused_computation.3 | convolution fusion | flops 4028497920 | bytes 10092544 | tf_op jit(solution)/shard_map/dot_general | solution.py:48
  77.5 5.9 convolution_convert_fusion.2
  83.4 41.2 %all-gather.8.cloned.1.call-done = bf16[2048,1024]{1,0:T(8,128)(2,1)} async-done(((bf16[128,1024]{1,0:T(8,128)(2,1)}), bf16[2048,1024]{1,0:T(8,128)(2,1)}) %all-gather.8.cloned.1.call-update) | async-done | bytes 4194320 | tf_op jit(solution)/shard_map/all_gather | solution.py:45
  124.7 7.2 convolution_convert_fusion
  131.9 19.8 %pad_maximum_fusion = bf16[2048,2880]{0,1:T(8,128)(2,1)} fusion(bf16[2048,960]{0,1:T(8,128)(2,1)S(1)} %convolution_convert_fusion, bf16[2048,960]{0,1:T(8,128)(2,1)S(1)} %copy-done.2, bf16[2048,960]{0,1:T(8,128)(2,1)S(1)} %copy-done.3), kind=kLoop, calls=%fused_computation | loop fusion | flops 35389440 | bytes 23592960 | tf_op jit(solution)/shard_map/concatenate | solution.py:51
  151.8 0.2 all-gather.10.cloned.1.call-start
  152.0 230.9 %reduce-scatter.3.cloned.1.call-done = bf16[256,2880]{0,1:T(8,128)(2,1)} async-done(((bf16[2048,2880]{0,1:T(8,128)(2,1)}), bf16[256,2880]{0,1:T(8,128)(2,1)}) %reduce-scatter.3.cloned.1.call-update) | async-done | bytes 1474576 | tf_op jit(solution)/shard_map/reduce_scatter | solution.py:50
  382.9 1.6 convert_element_type.31
  384.5 1.7 multiply_convert_fusion
  386.3 0.5 all-gather.12.cloned.1.call-update
  386.9 0.5 all-gather.14.cloned.1.call-update
  387.5 84.4 %all-gather.10.cloned.1.call-done = bf16[2048,960]{0,1:T(8,128)(2,1)} async-done(((bf16[256,960]{0,1:T(8,128)(2,1)}), bf16[2048,960]{0,1:T(8,128)(2,1)}) %all-gather.10.cloned.1.call-update) | async-done | bytes 3932176 | tf_op jit(solution)/shard_map/all_gather | solution.py:59
  471.9 8.9 %fusion.1 = f32[2048,1024]{1,0:T(8,128)} fusion(bf16[2048,960]{0,1:T(8,128)(2,1)} %all-gather.10.cloned.1.call-done, bf16[1024,960]{0,1:T(8,128)(2,1)S(1)} %copy-done), kind=kOutput, calls=%fused_computation.22 | convolution fusion | flops 4026531840 | bytes 14286848 | tf_op jit(solution)/shard_map/dot_general | solution.py:16
  480.8 78.6 %all-gather.12.cloned.1.call-done = bf16[2048,960]{0,1:T(8,128)(2,1)} async-done(((bf16[256,960]{0,1:T(8,128)(2,1)}), bf16[2048,960]{0,1:T(8,128)(2,1)}) %all-gather.12.cloned.1.call-update) | async-done | bytes 3932176 | tf_op jit(solution)/shard_map/all_gather | solution.py:60
  559.4 11.6 %add_convert_fusion = bf16[2048,1024]{1,0:T(8,128)(2,1)} fusion(f32[2048,1024]{1,0:T(8,128)} %fusion.1, bf16[2048,960]{0,1:T(8,128)(2,1)} %all-gather.12.cloned.1.call-done, bf16[1024,960]{0,1:T(8,128)(2,1)} %param.10), kind=kOutput, calls=%fused_computation.1 | convolution fusion | flops 4030726144 | bytes 18481152 | tf_op jit(solution)/shard_map/dot_general | solution.py:16
  571.1 9.1 %convert_bitcast_fusion = bf16[1024,960]{0,1:T(8,128)(2,1)} fusion(bf16[2048,960]{0,1:T(8,128)(2,1)} %all-gather.12.cloned.1.call-done, bf16[2048,1024]{1,0:T(8,128)(2,1)} %all-gather.6.cloned.1.call-done), kind=kOutput, calls=%fused_computation.5 | convolution fusion | flops 4027514880 | bytes 10092544 | tf_op jit(solution)/shard_map/dot_general | solution.py:10
  580.2 5.4 convert_bitcast_fusion.1
  585.6 61.3 %all-gather.14.cloned.1.call-done = bf16[2048,960]{0,1:T(8,128)(2,1)} async-done(((bf16[256,960]{0,1:T(8,128)(2,1)}), bf16[2048,960]{0,1:T(8,128)(2,1)}) %all-gather.14.cloned.1.call-update) | async-done | bytes 3932176 | tf_op jit(solution)/shard_map/all_gather | solution.py:58
  646.9 9.0 %convolution_convert_fusion.3 = bf16[960,1024]{1,0:T(8,128)(2,1)} fusion(bf16[2048,960]{0,1:T(8,128)(2,1)} %all-gather.14.cloned.1.call-done, bf16[2048,1024]{1,0:T(8,128)(2,1)} %all-gather.8.cloned.1.call-done), kind=kOutput, calls=%fused_computation.7 | convolution fusion | flops 4027514880 | bytes 10092544 | tf_op jit(solution)/shard_map/dot_general | solution.py:10
  655.9 77.3 %reduce-scatter.5.cloned.1.call-done = bf16[128,1024]{1,0:T(8,128)(2,1)} async-done(((bf16[2048,1024]{1,0:T(8,128)(2,1)}), bf16[128,1024]{1,0:T(8,128)(2,1)}) %reduce-scatter.5.cloned.1.call-update) | async-done | bytes 262160 | tf_op jit(solution)/shard_map/reduce_scatter | solution.py:65
  (26 shorter events, 0.4 us)
Async XLA Ops:
  7.2 70.3 %copy-start = (bf16[1024,960]{0,1:T(8,128)(2,1)S(1)}, bf16[1024,960]{0,1:T(8,128)(2,1)}, u32[]{:S(2)}) copy-start(bf16[1024,960]{0,1:T(8,128)(2,1)} %param.9) | copy-start | bytes 5898244
  7.2 61.2 %all-gather.6.cloned.1.call-start = ((), (), s32[]{:S(2)}) async-start(), calls=%async_computation.2 | async-start | bytes 4456448 | tf_op jit(solution)/shard_map/all_gather | solution.py:44
  7.9 116.7 %all-gather.8.cloned.1.call-start = ((), (), s32[]{:S(2)}) async-start(), calls=%async_computation.3 | async-start | bytes 4456448 | tf_op jit(solution)/shard_map/all_gather | solution.py:45
  10.5 372.4 %reduce-scatter.3.cloned.1.call-start = ((), (), s32[]{:S(2)}) async-start(), calls=%async_computation.4 | async-start | bytes 13271040 | tf_op jit(solution)/shard_map/reduce_scatter | solution.py:50
  68.4 9.1 %copy-start.4 = (bf16[2048,1024]{1,0:T(8,128)(2,1)S(1)}, bf16[2048,1024]{1,0:T(8,128)(2,1)}, u32[]{:S(2)}) copy-start(bf16[2048,1024]{1,0:T(8,128)(2,1)} %all-gather.6.cloned.1.call-done) | copy-start | bytes 12582916
  124.7 7.2 copy-start.2
  124.7 7.2 copy-start.3
  151.8 320.1 %all-gather.10.cloned.1.call-start = ((), (), s32[]{:S(2)}) async-start(), calls=%async_computation.5 | async-start | bytes 4423680 | tf_op jit(solution)/shard_map/all_gather | solution.py:59
  386.3 173.1 %all-gather.12.cloned.1.call-start = ((), (), s32[]{:S(2)}) async-start(), calls=%async_computation.6 | async-start | bytes 4423680 | tf_op jit(solution)/shard_map/all_gather | solution.py:60
  386.9 260.0 %all-gather.14.cloned.1.call-start = ((), (), s32[]{:S(2)}) async-start(), calls=%async_computation.8 | async-start | bytes 4423680 | tf_op jit(solution)/shard_map/all_gather | solution.py:58
  387.5 345.8 %reduce-scatter.5.cloned.1.call-start = ((), (), s32[]{:S(2)}) async-start(), calls=%async_computation.7 | async-start | bytes 4456448 | tf_op jit(solution)/shard_map/reduce_scatter | solution.py:65
  571.1 9.1 %copy-start.5 = (bf16[2048,1024]{1,0:T(8,128)(2,1)S(1)}, bf16[2048,1024]{1,0:T(8,128)(2,1)}, u32[]{:S(2)}) copy-start(bf16[2048,1024]{1,0:T(8,128)(2,1)} %all-gather.6.cloned.1.call-done) | copy-start | bytes 12582916
  571.1 9.1 %copy-start.6 = (bf16[2048,960]{0,1:T(8,128)(2,1)S(1)}, bf16[2048,960]{0,1:T(8,128)(2,1)}, u32[]{:S(2)}) copy-start(bf16[2048,960]{0,1:T(8,128)(2,1)} %all-gather.10.cloned.1.call-done) | copy-start | bytes 11796484
  646.9 86.3 %copy-start.1 = (bf16[1024,960]{0,1:T(8,128)(2,1)S(1)}, bf16[1024,960]{0,1:T(8,128)(2,1)}, u32[]{:S(2)}) copy-start(bf16[1024,960]{0,1:T(8,128)(2,1)} %param.9) | copy-start | bytes 5898244
Sparse Core Ops, SparseCore 0:
  10.5 57.8 all-gather.5
  71.5 53.1 all-gather.7
  151.9 230.9 reduce-scatter.2
  386.4 85.4 all-gather.9
  473.9 85.4 all-gather.11
  561.4 85.4 all-gather.13
  651.5 81.6 reduce-scatter.4
where the time goes:
time: 740 us
  waiting for transfers between devices  633 us (86%)
  matrix products  66.3 us (9%)
  other arithmetic  25.7 us (3%)
  between operations  14.2 us (2%)
    reduce_scatter x1, waiting for transfers between devices, shards(): lax.psum_scatter(jnp.concatenate([gate_part, up_part, back_part], axis=1)...  231 us
    all_gather x1, waiting for transfers between devices, shards(): lax.all_gather(gate_share, 'row', axis=0, tiled=True)  84.4 us
    all_gather x1, waiting for transfers between devices, shards(): lax.all_gather(up_share, 'row', axis=0, tiled=True)  78.6 us
    reduce_scatter x1, waiting for transfers between devices, shards(): lax.psum_scatter((contract_cols(d_gate, w_gate) + contract_cols(d_up, w_u...  77.3 us
    all_gather x1, waiting for transfers between devices, shards(): lax.all_gather(hidden_share, 'row', axis=0, tiled=True)  61.3 us
    all_gather x1, waiting for transfers between devices, shards(): lax.all_gather(activations, 'col', axis=0, tiled=True)  57.9 us
    all_gather x1, waiting for transfers between devices, shards(): lax.all_gather(live_grad, 'col', axis=0, tiled=True)  41.2 us
    dot_general x3, matrix products, contract_cols(): lax.dot_general(left, right, (((1,), (1,)), ((), ())), preferred_element_...  27.8 us
  transfers between devices with their start and end apart: 7, of which 7 were waited for; matrix products, arithmetic and copies ran while one was open for 8% of the time, Pallas kernels for 0%

commit v1 on v0

--- a/solution.py
+++ b/solution.py
@@ -4,6 +4,11 @@
 from jax.sharding import PartitionSpec as P
 
 TILE = 64
+
+
+def gather_over(shard, axis, along):
+    outgoing = jnp.stack([shard] * lax.axis_size(axis))
+    return jnp.concatenate(lax.all_to_all(outgoing, axis, 0, 0), axis=along)
 
 
 def contract_rows(left, right):
@@ -56,7 +61,7 @@
     hidden_share, gate_share, up_share = swiglu_back(totals, columns)
     hidden, d_gate, d_up = (
         lax.all_gather(hidden_share, "row", axis=0, tiled=True),
-        lax.all_gather(gate_share, "row", axis=0, tiled=True),
+        gather_over(gate_share, "row", 0),
         lax.all_gather(up_share, "row", axis=0, tiled=True),
     )
     grad_gate = contract_rows(inputs_all, d_gate).astype(jnp.bfloat16)

time: 740 us -> 691 us (0.934)
  waiting for transfers between devices: 633 us -> 493 us
  blocking collectives: 0 us -> 91.4 us
    all_to_all x0 -> x1, blocking collectives: none -> 91.4 us  [gather_over(): return jnp.concatenate(lax.all_to_all(outgoing, axis, 0, 0), axis=along)]
    all_gather x1 -> x0, waiting for transfers between devices: 84.4 us -> none  [shards(): lax.all_gather(gate_share, 'row', axis=0, tiled=True)]
    all_gather x1, waiting for transfers between devices: 78.6 us -> 22.6 us  [shards(): lax.all_gather(up_share, 'row', axis=0, tiled=True)]
  transfers between devices with their start and end apart: 7 -> 6, of which waited for: 7 -> 6; matrix products, arithmetic and copies ran while one was open for 8% -> 9% of each run, Pallas kernels for 0% -> 0%
where the time goes in v1:
time: 691 us
  waiting for transfers between devices  493 us (71%)
  blocking collectives  91.4 us (13%)
  matrix products  64.2 us (9%)
  other arithmetic  25.4 us (4%)
  between operations  14.2 us (2%)
    reduce_scatter x1, waiting for transfers between devices, shards(): lax.psum_scatter(jnp.concatenate([gate_part, up_part, back_part], axis=1)...  231 us
    all_to_all x1, blocking collectives, gather_over(): return jnp.concatenate(lax.all_to_all(outgoing, axis, 0, 0), axis=along)  91.4 us
    reduce_scatter x1, waiting for transfers between devices, shards(): lax.psum_scatter((contract_cols(d_gate, w_gate) + contract_cols(d_up, w_u...  77.1 us
    all_gather x1, waiting for transfers between devices, shards(): lax.all_gather(hidden_share, 'row', axis=0, tiled=True)  61.5 us
    all_gather x1, waiting for transfers between devices, shards(): lax.all_gather(activations, 'col', axis=0, tiled=True)  57.9 us
    all_gather x1, waiting for transfers between devices, shards(): lax.all_gather(live_grad, 'col', axis=0, tiled=True)  41.2 us
    dot_general x3, matrix products, contract_cols(): lax.dot_general(left, right, (((1,), (1,)), ((), ())), preferred_element_...  25.7 us
    dot_general x3, matrix products, contract_rows(): lax.dot_general(left, right, (((0,), (0,)), ((), ())), preferred_element_...  23.5 us
  transfers between devices with their start and end apart: 6, of which 6 were waited for; matrix products, arithmetic and copies ran while one was open for 9% of the time, Pallas kernels for 0%

profile of v1, /device:TPU:0, one launch (start us, length us, event | category | flops | bytes accessed | tf_op | source)
XLA Modules:
  0.0 691.0 jit_solution(12483281980457821865)
XLA Ops:
  7.2 0.7 all-gather.5.cloned.1.call-update
  8.0 0.7 select_reduce_fusion
  8.7 1.7 broadcast_select_fusion
  10.6 57.9 %all-gather.5.cloned.1.call-done = bf16[2048,1024]{1,0:T(8,128)(2,1)} async-done(((bf16[128,1024]{1,0:T(8,128)(2,1)}), bf16[2048,1024]{1,0:T(8,128)(2,1)}) %all-gather.5.cloned.1.call-update) | async-done | bytes 4194320 | tf_op jit(solution)/shard_map/all_gather | solution.py:49
  68.4 9.1 %convolution_convert_fusion.1 = bf16[2048,960]{0,1:T(8,128)(2,1)} fusion(bf16[2048,1024]{1,0:T(8,128)(2,1)} %all-gather.5.cloned.1.call-done, bf16[1024,960]{0,1:T(8,128)(2,1)} %param.10), kind=kOutput, calls=%fused_computation.3 | convolution fusion | flops 4028497920 | bytes 10092544 | tf_op jit(solution)/shard_map/dot_general | solution.py:53
  77.5 5.9 convolution_convert_fusion.2
  83.4 41.2 %all-gather.7.cloned.1.call-done = bf16[2048,1024]{1,0:T(8,128)(2,1)} async-done(((bf16[128,1024]{1,0:T(8,128)(2,1)}), bf16[2048,1024]{1,0:T(8,128)(2,1)}) %all-gather.7.cloned.1.call-update) | async-done | bytes 4194320 | tf_op jit(solution)/shard_map/all_gather | solution.py:50
  124.7 7.2 %convolution_convert_fusion = bf16[2048,960]{0,1:T(8,128)(2,1)S(1)} fusion(bf16[2048,1024]{1,0:T(8,128)(2,1)} %all-gather.7.cloned.1.call-done, bf16[960,1024]{1,0:T(8,128)(2,1)} %param.11), kind=kOutput, calls=%fused_computation.2 | convolution fusion | flops 4028497920 | bytes 10092544 | tf_op jit(solution)/shard_map/dot_general | solution.py:21
  131.9 19.9 %pad_maximum_fusion = bf16[2048,2880]{0,1:T(8,128)(2,1)} fusion(bf16[2048,960]{0,1:T(8,128)(2,1)S(1)} %convolution_convert_fusion, bf16[2048,960]{0,1:T(8,128)(2,1)S(1)} %copy-done.3, bf16[2048,960]{0,1:T(8,128)(2,1)S(1)} %copy-done.4), kind=kLoop, calls=%fused_computation | loop fusion | flops 35389440 | bytes 23592960 | tf_op jit(solution)/shard_map/concatenate | solution.py:56
  152.0 230.9 %reduce-scatter.3.cloned.1.call-done = bf16[256,2880]{0,1:T(8,128)(2,1)} async-done(((bf16[2048,2880]{0,1:T(8,128)(2,1)}), bf16[256,2880]{0,1:T(8,128)(2,1)}) %reduce-scatter.3.cloned.1.call-update) | async-done | bytes 1474576 | tf_op jit(solution)/shard_map/reduce_scatter | solution.py:55
  383.0 1.6 convert_element_type.31
  384.6 1.5 multiply_convert_fusion
  386.1 0.5 all-gather.11.cloned.1.call-update
  387.0 91.4 %all_to_all.5 = bf16[8,256,960]{1,2,0:T(8,128)(2,1)S(1)} all-to-all(bf16[8,256,960]{1,2,0:T(8,128)(2,1)S(1)} %stack.2), channel_id=1, replica_groups=mesh['row'=8,'col'=16] {'row'}, dimensions={0} | all-to-all | bytes 7864320 | tf_op jit(solution)/shard_map/all_to_all | solution.py:11
  478.4 0.5 copy.13
  478.9 1.9 copy-done.2
  480.8 6.8 fusion.1
  487.6 22.6 %all-gather.9.cloned.1.call-done = bf16[2048,960]{0,1:T(8,128)(2,1)} async-done(((bf16[256,960]{0,1:T(8,128)(2,1)}), bf16[2048,960]{0,1:T(8,128)(2,1)}) %all-gather.9.cloned.1.call-update) | async-done | bytes 3932176 | tf_op jit(solution)/shard_map/all_gather | solution.py:65
  510.3 11.6 %add_convert_fusion = bf16[2048,1024]{1,0:T(8,128)(2,1)} fusion(f32[2048,1024]{1,0:T(8,128)} %fusion.1, bf16[2048,960]{0,1:T(8,128)(2,1)} %all-gather.9.cloned.1.call-done, bf16[1024,960]{0,1:T(8,128)(2,1)} %param.10), kind=kOutput, calls=%fused_computation.1 | convolution fusion | flops 4030726144 | bytes 18481152 | tf_op jit(solution)/shard_map/dot_general | solution.py:21
  522.0 9.1 %convert_bitcast_fusion.1 = bf16[1024,960]{0,1:T(8,128)(2,1)} fusion(bf16[2048,960]{0,1:T(8,128)(2,1)} %bitcast.24, bf16[2048,1024]{1,0:T(8,128)(2,1)} %all-gather.5.cloned.1.call-done), kind=kOutput, calls=%fused_computation.6 | convolution fusion | flops 4027514880 | bytes 10092544 | tf_op jit(solution)/shard_map/dot_general | solution.py:15
  531.1 5.4 convert_bitcast_fusion
  536.5 61.5 %all-gather.11.cloned.1.call-done = bf16[2048,960]{0,1:T(8,128)(2,1)} async-done(((bf16[256,960]{0,1:T(8,128)(2,1)}), bf16[2048,960]{0,1:T(8,128)(2,1)}) %all-gather.11.cloned.1.call-update) | async-done | bytes 3932176 | tf_op jit(solution)/shard_map/all_gather | solution.py:63
  598.0 9.0 %convolution_convert_fusion.3 = bf16[960,1024]{1,0:T(8,128)(2,1)} fusion(bf16[2048,960]{0,1:T(8,128)(2,1)} %all-gather.11.cloned.1.call-done, bf16[2048,1024]{1,0:T(8,128)(2,1)} %all-gather.7.cloned.1.call-done), kind=kOutput, calls=%fused_computation.7 | convolution fusion | flops 4027514880 | bytes 10092544 | tf_op jit(solution)/shard_map/dot_general | solution.py:15
  607.0 77.1 %reduce-scatter.5.cloned.1.call-done = bf16[128,1024]{1,0:T(8,128)(2,1)} async-done(((bf16[2048,1024]{1,0:T(8,128)(2,1)}), bf16[128,1024]{1,0:T(8,128)(2,1)}) %reduce-scatter.5.cloned.1.call-update) | async-done | bytes 262160 | tf_op jit(solution)/shard_map/reduce_scatter | solution.py:70
  (28 shorter events, 0.8 us)
Async XLA Ops:
  7.2 70.3 %copy-start = (bf16[1024,960]{0,1:T(8,128)(2,1)S(1)}, bf16[1024,960]{0,1:T(8,128)(2,1)}, u32[]{:S(2)}) copy-start(bf16[1024,960]{0,1:T(8,128)(2,1)} %param.9) | copy-start | bytes 5898244
  7.2 61.2 %all-gather.5.cloned.1.call-start = ((), (), s32[]{:S(2)}) async-start(), calls=%async_computation.3 | async-start | bytes 4456448 | tf_op jit(solution)/shard_map/all_gather | solution.py:49
  7.9 116.7 %all-gather.7.cloned.1.call-start = ((), (), s32[]{:S(2)}) async-start(), calls=%async_computation.4 | async-start | bytes 4456448 | tf_op jit(solution)/shard_map/all_gather | solution.py:50
  10.5 372.4 %reduce-scatter.3.cloned.1.call-start = ((), (), s32[]{:S(2)}) async-start(), calls=%async_computation.5 | async-start | bytes 13271040 | tf_op jit(solution)/shard_map/reduce_scatter | solution.py:55
  68.4 9.1 %copy-start.5 = (bf16[2048,1024]{1,0:T(8,128)(2,1)S(1)}, bf16[2048,1024]{1,0:T(8,128)(2,1)}, u32[]{:S(2)}) copy-start(bf16[2048,1024]{1,0:T(8,128)(2,1)} %all-gather.5.cloned.1.call-done) | copy-start | bytes 12582916
  124.7 7.2 %copy-start.3 = (bf16[2048,960]{0,1:T(8,128)(2,1)S(1)}, bf16[2048,960]{0,1:T(8,128)(2,1)}, u32[]{:S(2)}) copy-start(bf16[2048,960]{0,1:T(8,128)(2,1)} %convolution_convert_fusion.1) | copy-start | bytes 11796484
  124.7 7.2 %copy-start.4 = (bf16[2048,960]{0,1:T(8,128)(2,1)S(1)}, bf16[2048,960]{0,1:T(8,128)(2,1)}, u32[]{:S(2)}) copy-start(bf16[2048,960]{0,1:T(8,128)(2,1)} %convolution_convert_fusion.2) | copy-start | bytes 11796484
  151.8 358.5 %all-gather.9.cloned.1.call-start = ((), (), s32[]{:S(2)}) async-start(), calls=%async_computation.6 | async-start | bytes 4423680 | tf_op jit(solution)/shard_map/all_gather | solution.py:65
  386.1 212.0 %all-gather.11.cloned.1.call-start = ((), (), s32[]{:S(2)}) async-start(), calls=%async_computation.8 | async-start | bytes 4423680 | tf_op jit(solution)/shard_map/all_gather | solution.py:63
  386.7 297.5 %reduce-scatter.5.cloned.1.call-start = ((), (), s32[]{:S(2)}) async-start(), calls=%async_computation.7 | async-start | bytes 4456448 | tf_op jit(solution)/shard_map/reduce_scatter | solution.py:70
  478.9 1.9 copy-start.2
  522.0 9.2 %copy-start.6 = (bf16[2048,1024]{1,0:T(8,128)(2,1)S(1)}, bf16[2048,1024]{1,0:T(8,128)(2,1)}, u32[]{:S(2)}) copy-start(bf16[2048,1024]{1,0:T(8,128)(2,1)} %all-gather.5.cloned.1.call-done) | copy-start | bytes 12582916
  522.0 9.1 %copy-start.7 = (bf16[2048,960]{0,1:T(8,128)(2,1)S(1)}, bf16[2048,960]{0,1:T(8,128)(2,1)}, u32[]{:S(2)}) copy-start(bf16[2048,960]{0,1:T(8,128)(2,1)} %all-gather.9.cloned.1.call-done) | copy-start | bytes 11796484
  598.0 86.1 %copy-start.1 = (bf16[1024,960]{0,1:T(8,128)(2,1)S(1)}, bf16[1024,960]{0,1:T(8,128)(2,1)}, u32[]{:S(2)}) copy-start(bf16[1024,960]{0,1:T(8,128)(2,1)} %param.9) | copy-start | bytes 5898244
Sparse Core Ops, SparseCore 0:
  10.5 57.8 all-gather.4
  71.5 53.1 all-gather.6
  151.9 230.9 reduce-scatter.2
  386.2 124.0 all-gather.8
  512.3 85.6 all-gather.10
  602.5 81.6 reduce-scatter.4
